TPU v7x, 32 devices: a whole 2x2x4 slice. The times are simulated.
32 devices in a mesh: dp: 2 (over x), row: 4 (over z), col: 4 (over y, core).
Axes of the slice: x: 2, y: 2, z: 4, core: 2. Of those that a mesh axis runs over, the one named last changes fastest.
Arguments:
- inputs: bfloat16 [1458, 1152], P('dp', 'row'), may hold values from -40 to 40
- pre_gain: float32 [1152], P('row'), may hold values from 0.5 to 1.5
- pre_shift: float32 [1152], P('row'), may hold values from -1.5 to 1.5
- joint_weight: bfloat16 [1152, 3456], P('row', 'col'), may hold values from -0.1875 to 0.1875
- joint_bias: float32 [4, 4, 144], P('col', 'row'), may hold values from -0.5 to 0.5
- merge_weight: bfloat16 [1152, 1152], P('col', 'row'), may hold values from -4 to 4
- merge_bias: float32 [1152], P('row'), may hold values from -2.5 to 2.5
- mid_gain: float32 [1152], P('row'), may hold values from 0.5 to 1.5
- mid_shift: float32 [1152], P('row'), may hold values from -1.5 to 1.5
- expand_weight: bfloat16 [1152, 4304], P('row', 'col'), may hold values from -0.1875 to 0.1875
- expand_bias: float32 [4304], P('col'), may hold values from -1.5 to 1.5
- reduce_weight: bfloat16 [4304, 1152], P('col', 'row'), may hold values from -0.09375 to 0.09375
- reduce_bias: float32 [1152], P('row'), may hold values from -2.5 to 2.5
- cotangent: bfloat16 [1458, 1152], P('dp', 'row'), may hold values from -6 to 6
Outputs:
- outputs: bfloat16 [1458, 1152], P('dp', 'row')
- inputs_grad: float32 [1458, 1152], P('dp', 'row')
- pre_gain_grad: float32 [1152], P('row')
- pre_shift_grad: float32 [1152], P('row')
- joint_weight_grad: float32 [1152, 3456], P('row', 'col')
- joint_bias_grad: float32 [4, 4, 144], P('col', 'row')
- merge_weight_grad: float32 [1152, 1152], P('col', 'row')
- merge_bias_grad: float32 [1152], P('row')
- mid_gain_grad: float32 [1152], P('row')
- mid_shift_grad: float32 [1152], P('row')
- expand_weight_grad: float32 [1152, 4304], P('row', 'col')
- expand_bias_grad: float32 [4304], P('col')
- reduce_weight_grad: float32 [4304, 1152], P('col', 'row')
- reduce_bias_grad: float32 [1152], P('row')
All inputs are finite; a program needn't handle non-finite values.
Results may differ from a plain program's by a relative error of at most 0.015.
Values may be sent and summed in bfloat16 or wider, within the bound.
No kernel may reach another device: no remote copies, remote signals or barrier semaphores. Data moves between devices by JAX's collectives and lax.ppermute only.
A program may use at most 64 MiB of HBM per device.

v0:
```python
import jax
import jax.numpy as jnp
from jax import lax
from jax.sharding import PartitionSpec as P

D = 1152
SEQ = 729
NORM_EPSILON = 1e-06
TANH_SLOPE = 0.7978845608028654
CUBIC_TERM = 0.044715


def gelu_value(preact):
    return (
        0.5
        * preact
        * (1.0 + jnp.tanh(TANH_SLOPE * (preact + CUBIC_TERM * preact * preact * preact)))
    )


def gelu_slope(preact):
    inner_tanh = jnp.tanh(TANH_SLOPE * (preact + CUBIC_TERM * preact * preact * preact))
    return 0.5 * (1.0 + inner_tanh) + 0.5 * preact * (
        1.0 - inner_tanh * inner_tanh
    ) * TANH_SLOPE * (1.0 + 3.0 * CUBIC_TERM * preact * preact)


def contract_rows(left, right):
    return lax.dot_general(
        left, right, (((0,), (0,)), ((), ())), preferred_element_type=jnp.float32
    )


def contract_cols(left, right):
    return lax.dot_general(
        left, right, (((1,), (1,)), ((), ())), preferred_element_type=jnp.float32
    )


def row_totals(first, second):
    return lax.psum((first, second), "row")


def col_total(partial_sum):
    return lax.psum(partial_sum, "col")


def ff_total(partial_sum):
    return lax.psum(partial_sum, "row")


def norm_forward(values, norm_gain, norm_shift):
    first, second = row_totals(
        jnp.sum(values, axis=-1, keepdims=True), jnp.sum(values * values, axis=-1, keepdims=True)
    )
    row_mean = first / D
    row_var = second / D - row_mean * row_mean
    inv_scale = lax.rsqrt(row_var + NORM_EPSILON)
    unit_rows = (values - row_mean) * inv_scale
    return (unit_rows, inv_scale, unit_rows * norm_gain + norm_shift)


def norm_backward(upstream, unit_rows, inv_scale, norm_gain):
    scaled = upstream * norm_gain
    first, second = row_totals(
        jnp.sum(scaled, axis=-1, keepdims=True), jnp.sum(scaled * unit_rows, axis=-1, keepdims=True)
    )
    return inv_scale * (scaled - first / D - unit_rows * (second / D))


def attend_image(query_rows, key_rows, value_rows):
    factor = query_rows.shape[-1] ** (-0.5)
    scores = (
        jnp.einsum("qhd,khd->hqk", query_rows, key_rows, preferred_element_type=jnp.float32)
        * factor
    )
    totals = jnp.log(jnp.sum(jnp.exp(scores), axis=-1))
    softmax_rows = jnp.exp(scores - totals[..., None]).astype(jnp.bfloat16)
    context = jnp.einsum(
        "hqk,khd->qhd", softmax_rows, value_rows, preferred_element_type=jnp.float32
    )
    return (context.astype(jnp.bfloat16), totals)


def attend_back(query_rows, key_rows, value_rows, context, totals, upstream):
    factor = query_rows.shape[-1] ** (-0.5)
    scores = (
        jnp.einsum("qhd,khd->hqk", query_rows, key_rows, preferred_element_type=jnp.float32)
        * factor
    )
    weights = jnp.exp(scores - totals[..., None])
    value_grad = jnp.einsum(
        "hqk,qhd->khd", weights.astype(jnp.bfloat16), upstream, preferred_element_type=jnp.float32
    )
    prob_grad = jnp.einsum("qhd,khd->hqk", upstream, value_rows, preferred_element_type=jnp.float32)
    row_delta = jnp.einsum("qhd,qhd->hq", upstream, context, preferred_element_type=jnp.float32)
    score_grad = (weights * (prob_grad - row_delta[..., None])).astype(jnp.bfloat16)
    query_grad = (
        jnp.einsum("hqk,khd->qhd", score_grad, key_rows, preferred_element_type=jnp.float32)
        * factor
    )
    key_grad = (
        jnp.einsum("hqk,qhd->khd", score_grad, query_rows, preferred_element_type=jnp.float32)
        * factor
    )
    return (query_grad, key_grad, value_grad)


def body(
    inputs,
    pre_gain,
    pre_shift,
    joint_weight,
    joint_bias,
    merge_weight,
    merge_bias,
    mid_gain,
    mid_shift,
    expand_weight,
    expand_bias,
    reduce_weight,
    reduce_bias,
    cotangent,
):
    token_count = inputs.shape[0]
    image_count = token_count // SEQ
    local_heads = joint_bias.shape[1]
    head_size = joint_bias.shape[2] // 2
    residual = inputs.astype(jnp.float32)
    unit_first, scale_first, normed_first = norm_forward(residual, pre_gain, pre_shift)
    normed_first = normed_first.astype(jnp.bfloat16)
    joint_part = jnp.dot(normed_first, joint_weight, preferred_element_type=jnp.float32)
    joint_sum = lax.psum_scatter(joint_part, "row", scatter_dimension=1, tiled=True)
    bias_pairs = joint_bias.reshape(local_heads, 2 * head_size)
    bias_rows = jnp.concatenate(
        [
            bias_pairs[:, :head_size],
            jnp.zeros((local_heads, head_size), jnp.float32),
            bias_pairs[:, head_size:],
        ],
        axis=1,
    ).reshape(-1)
    joint_rows = (joint_sum + bias_rows).astype(jnp.bfloat16)
    per_head = joint_rows.reshape(image_count, SEQ, local_heads, 3 * head_size)
    query_rows = per_head[..., :head_size]
    key_rows = per_head[..., head_size : 2 * head_size]
    value_rows = per_head[..., 2 * head_size :]
    context, totals = lax.map(
        lambda packed: attend_image(packed[0], packed[1], packed[2]),
        (query_rows, key_rows, value_rows),
    )
    context_flat = context.reshape(token_count, local_heads * head_size)
    context_group = lax.all_gather(context_flat, "row", axis=1, tiled=True)
    mixed_first = (
        residual
        + col_total(jnp.dot(context_group, merge_weight, preferred_element_type=jnp.float32))
        + merge_bias
    )
    unit_second, scale_second, normed_second = norm_forward(mixed_first, mid_gain, mid_shift)
    normed_second = normed_second.astype(jnp.bfloat16)
    hidden_pre = (
        ff_total(jnp.dot(normed_second, expand_weight, preferred_element_type=jnp.float32))
        + expand_bias
    )
    active = gelu_value(hidden_pre).astype(jnp.bfloat16)
    mixed_second = (
        mixed_first
        + col_total(jnp.dot(active, reduce_weight, preferred_element_type=jnp.float32))
        + reduce_bias
    )
    outputs = mixed_second.astype(jnp.bfloat16)
    grad_out = cotangent.astype(jnp.float32)
    reduce_weight_grad = contract_rows(active, cotangent)
    reduce_bias_grad = jnp.sum(grad_out, axis=0)
    hidden_grad = (
        ff_total(contract_cols(cotangent, reduce_weight)) * gelu_slope(hidden_pre)
    ).astype(jnp.bfloat16)
    expand_weight_grad = contract_rows(normed_second, hidden_grad)
    expand_bias_grad = jnp.sum(hidden_grad, axis=0, dtype=jnp.float32)
    normed_second_grad = col_total(contract_cols(hidden_grad, expand_weight))
    mid_gain_grad = jnp.sum(normed_second_grad * unit_second, axis=0)
    mid_shift_grad = jnp.sum(normed_second_grad, axis=0)
    mixed_grad = grad_out + norm_backward(normed_second_grad, unit_second, scale_second, mid_gain)
    mixed_low = mixed_grad.astype(jnp.bfloat16)
    merge_weight_grad = contract_rows(context_group, mixed_low)
    merge_bias_grad = jnp.sum(mixed_grad, axis=0)
    context_grad = lax.psum_scatter(
        contract_cols(mixed_low, merge_weight), "row", scatter_dimension=1, tiled=True
    ).astype(jnp.bfloat16)
    context_grad = context_grad.reshape(image_count, SEQ, local_heads, head_size)
    query_grad, key_grad, value_grad = lax.map(
        lambda packed: attend_back(
            packed[0], packed[1], packed[2], packed[3], packed[4], packed[5]
        ),
        (query_rows, key_rows, value_rows, context, totals, context_grad),
    )
    joint_grad = (
        jnp.concatenate([query_grad, key_grad, value_grad], axis=-1)
        .astype(jnp.bfloat16)
        .reshape(token_count, 3 * local_heads * head_size)
    )
    joint_bias_grad = jnp.concatenate(
        [jnp.sum(query_grad, axis=(0, 1)), jnp.sum(value_grad, axis=(0, 1))], axis=-1
    ).reshape(1, local_heads, 2 * head_size)
    joint_group = lax.all_gather(joint_grad, "row", axis=1, tiled=True)
    joint_weight_grad = contract_rows(normed_first, joint_group)
    normed_first_grad = col_total(contract_cols(joint_group, joint_weight))
    pre_gain_grad = jnp.sum(normed_first_grad * unit_first, axis=0)
    pre_shift_grad = jnp.sum(normed_first_grad, axis=0)
    inputs_grad = mixed_grad + norm_backward(normed_first_grad, unit_first, scale_first, pre_gain)
    (
        reduce_weight_grad,
        reduce_bias_grad,
        expand_weight_grad,
        expand_bias_grad,
        mid_gain_grad,
        mid_shift_grad,
        joint_weight_grad,
        joint_bias_grad,
        merge_weight_grad,
        merge_bias_grad,
        pre_gain_grad,
        pre_shift_grad,
    ) = lax.psum(
        (
            reduce_weight_grad,
            reduce_bias_grad,
            expand_weight_grad,
            expand_bias_grad,
            mid_gain_grad,
            mid_shift_grad,
            joint_weight_grad,
            joint_bias_grad,
            merge_weight_grad,
            merge_bias_grad,
            pre_gain_grad,
            pre_shift_grad,
        ),
        "dp",
    )
    return (
        outputs,
        inputs_grad,
        pre_gain_grad,
        pre_shift_grad,
        joint_weight_grad,
        joint_bias_grad,
        merge_weight_grad,
        merge_bias_grad,
        mid_gain_grad,
        mid_shift_grad,
        expand_weight_grad,
        expand_bias_grad,
        reduce_weight_grad,
        reduce_bias_grad,
    )


def solution(mesh):
    in_specs = (
        P("dp", "row"),
        P("row"),
        P("row"),
        P("row", "col"),
        P("col", "row", None),
        P("col", "row"),
        P("row"),
        P("row"),
        P("row"),
        P("row", "col"),
        P("col"),
        P("col", "row"),
        P("row"),
        P("dp", "row"),
    )
    out_specs = (
        P("dp", "row"),
        P("dp", "row"),
        P("row"),
        P("row"),
        P("row", "col"),
        P("col", "row", None),
        P("col", "row"),
        P("row"),
        P("row"),
        P("row"),
        P("row", "col"),
        P("col"),
        P("col", "row"),
        P("row"),
    )
    return jax.shard_map(body, mesh=mesh, in_specs=in_specs, out_specs=out_specs, check_vma=False)
```

profile of v0, /device:TPU:0, one launch (start us, length us, event | category | flops | bytes accessed | tf_op | source)
XLA Modules:
  0.0 673.6 jit_solution(1483904082346468682)
XLA Ops:
  8.5 13.7 %all-reduce.4 = (f32[729,1]{0,1:T(1,128)S(1)}, f32[729,1]{0,1:T(1,128)S(1)}) all-reduce(f32[729,1]{0,1:T(1,128)S(1)} %broadcast_in_dim.57, f32[729,1]{0,1:T(1,128)S(1)} %broadcast_in_dim.58), channel_id=1, replica_groups=mesh['dp'=2,'row'=4,'col'=4] {'row'}, use_global_device_ids=true, to_apply=%region_1.0 | all-reduce | flops 1458 | bytes 11664 | tf_op jit(solution)/shard_map/psum | solution.py:41
  22.2 3.7 fusion.43
  26.3 50.8 %reduce-scatter.3.cloned.1.call-done = f32[729,216]{0,1:T(8,128)} async-done(((f32[729,864]{0,1:T(8,128)}), f32[729,216]{0,1:T(8,128)}) %reduce-scatter.3.cloned.1.call-update) | async-done | bytes 629872 | tf_op jit(solution)/shard_map/reduce_scatter | solution.py:133
  79.4 15.0 %all-gather = bf16[729,1,288]{0,2,1:T(8,128)(2,1)S(1)} all-gather(bf16[729,1,72]{0,2,1:T(8,128)(2,1)S(1)} %bitcast.72), channel_id=2, replica_groups=mesh['dp'=2,'row'=4,'col'=4] {'row'}, dimensions={2}, use_global_device_ids=true | all-gather | bytes 524880 | tf_op jit(solution)/shard_map/all_gather | solution.py:153
  96.7 4.1 fusion.59
  100.8 31.2 %all-reduce.14.cloned.1.call-done = f32[729,288]{0,1:T(8,128)} async-done(((f32[729,288]{0,1:T(8,128)}), f32[729,288]{0,1:T(8,128)}) %all-reduce.14.cloned.1.call-update) | async-done | bytes 839824 | tf_op jit(solution)/shard_map/psum | solution.py:45
  131.9 2.3 fusion.47
  134.2 11.8 %all-reduce.3 = (f32[729,1]{0,1:T(1,128)S(1)}, f32[729,1]{0,1:T(1,128)S(1)}) all-reduce(f32[729,1]{0,1:T(1,128)S(1)} %broadcast_in_dim.60, f32[729,1]{0,1:T(1,128)S(1)} %broadcast_in_dim.61), channel_id=1, replica_groups=mesh['dp'=2,'row'=4,'col'=4] {'row'}, use_global_device_ids=true, to_apply=%region_8.9 | all-reduce | flops 1458 | bytes 11664 | tf_op jit(solution)/shard_map/psum | solution.py:41
  146.1 4.1 fusion.46
  150.3 231.6 %all-reduce.20.cloned.1.call-done = (f32[729,1076]{0,1:T(8,128)}, f32[729,1076]{0,1:T(8,128)}) async-done(((f32[729,1076]{0,1:T(8,128)}, f32[729,1076]{0,1:T(8,128)}), (f32[729,1076]{0,1:T(8,128)}, f32[729,1076]{0,1:T(8,128)})) %all-reduce.20.cloned.1.call-update) | async-done | bytes 6275248 | tf_op jit(solution)/shard_map/psum | solution.py:49
  381.9 5.9 convert_reduce_fusion
  390.8 34.7 %all-reduce.16.cloned.1.call-done = f32[729,288]{0,1:T(8,128)} async-done(((f32[729,288]{0,1:T(8,128)}), f32[729,288]{0,1:T(8,128)}) %all-reduce.16.cloned.1.call-update) | async-done | bytes 839824 | tf_op jit(solution)/shard_map/psum | solution.py:45
  427.3 11.8 %all-reduce.2 = (f32[729,1]{0,1:T(1,128)S(1)}, f32[729,1]{0,1:T(1,128)S(1)}) all-reduce(f32[729,1]{0,1:T(1,128)S(1)} %broadcast_in_dim.63, f32[729,1]{0,1:T(1,128)S(1)} %broadcast_in_dim.62), channel_id=1, replica_groups=mesh['dp'=2,'row'=4,'col'=4] {'row'}, use_global_device_ids=true, to_apply=%region_18.19 | all-reduce | flops 1458 | bytes 11664 | tf_op jit(solution)/shard_map/psum | solution.py:41
  443.7 22.1 %reduce-scatter.5.cloned.1.call-done = f32[729,72]{0,1:T(8,128)} async-done(((f32[729,288]{0,1:T(8,128)}), f32[729,72]{0,1:T(8,128)}) %reduce-scatter.5.cloned.1.call-update) | async-done | bytes 209968 | tf_op jit(solution)/shard_map/reduce_scatter | solution.py:187
  471.1 3.4 fusion.58
  476.5 26.4 %all-gather.3.cloned.1.call-done = bf16[729,864]{0,1:T(8,128)(2,1)} async-done(((bf16[729,216]{0,1:T(8,128)(2,1)}), bf16[729,864]{0,1:T(8,128)(2,1)}) %all-gather.3.cloned.1.call-update) | async-done | bytes 1259728 | tf_op jit(solution)/shard_map/all_gather | solution.py:205
  502.9 2.9 fusion.61
  505.9 3.4 fusion.62
  512.2 38.8 %all-reduce.18.cloned.1.call-done = (f32[729,288]{0,1:T(8,128)}, f32[729,288]{0,1:T(8,128)}) async-done(((f32[729,288]{0,1:T(8,128)}, f32[729,288]{0,1:T(8,128)}), (f32[729,288]{0,1:T(8,128)}, f32[729,288]{0,1:T(8,128)})) %all-reduce.18.cloned.1.call-update) | async-done | bytes 1679632 | tf_op jit(solution)/shard_map/psum | solution.py:45
  552.7 9.0 %all-reduce.6 = (f32[288]{0:T(512)}, f32[288]{0:T(512)}, f32[1,1,144]{2,1,0:T(1,128)}, f32[288]{0:T(512)}, f32[288]{0:T(512)}, /*index=5*/f32[288]{0:T(512)}, f32[1076]{0:T(1024)}, f32[288]{0:T(512)}) all-reduce(f32[288]{0:T(512)S(1)} %get-tuple-element.64, ...), channel_id=1, replica_groups=mesh['dp'=2,'row'=4,'col'=4] {'dp'}, use_global_device_ids=true, to_apply=%region_26.27 | all-reduce | flops 2948 | bytes 23584 | tf_op jit(solution)/shard_map/psum | solution.py:224
  561.7 11.8 %all-reduce.1 = (f32[729,1]{0,1:T(1,128)S(1)}, f32[729,1]{0,1:T(1,128)S(1)}) all-reduce(f32[729,1]{0,1:T(1,128)S(1)} %broadcast_in_dim.65, f32[729,1]{0,1:T(1,128)S(1)} %broadcast_in_dim.64), channel_id=1, replica_groups=mesh['dp'=2,'row'=4,'col'=4] {'row'}, use_global_device_ids=true, to_apply=%region_24.25 | all-reduce | flops 1458 | bytes 11664 | tf_op jit(solution)/shard_map/psum | solution.py:41
  573.5 2.2 add_convert_fusion
  576.9 84.5 %all-reduce.22.cloned.1.call-done = (f32[288,864]{1,0:T(8,128)}, f32[288,288]{1,0:T(8,128)}, f32[288,1076]{1,0:T(8,128)}, f32[1076,288]{0,1:T(8,128)}) async-done(((f32[288,864]{1,0:T(8,128)}, f32[288,288]{1,0:T(8,128)}, f32[288,1076]{1,0:T(8,128)}, f32[1076,288]{0,1:T(8,128)}), (f32[288,864]{1,0:T(8,128)}, f32[288,288]{1,0:T(8,128)}, f32[288,1076]{1,0:T(8,128)}, ...) | async-done | bytes 3806224 | tf_op jit(solution)/shard_map/psum | solution.py:224
  661.5 2.4 copy.46
  (117 shorter events, 31.3 us)
Async XLA Ops:
  7.2 138.9 %copy-start = (bf16[288,1076]{1,0:T(8,128)(2,1)S(1)}, bf16[288,1076]{1,0:T(8,128)(2,1)}, u32[]{:S(2)}) copy-start(bf16[288,1076]{1,0:T(8,128)(2,1)} %param.23) | copy-start | bytes 1859332
  7.2 69.9 %reduce-scatter.3.cloned.1.call-start = ((), (), s32[]{:S(2)}) async-start(), calls=%async_computation.2 | async-start | bytes 3317760 | tf_op jit(solution)/shard_map/reduce_scatter | solution.py:133
  22.2 3.9 copy-start.28
  26.0 105.9 %all-reduce.14.cloned.1.call-start = ((), (), s32[]{:S(2)}) async-start(), calls=%async_computation.3 | async-start | bytes 1769472 | tf_op jit(solution)/shard_map/psum | solution.py:45
  78.3 16.9 %copy-start.18 = (bf16[288,288]{1,0:T(8,128)(2,1)S(1)}, bf16[288,288]{1,0:T(8,128)(2,1)}, u32[]{:S(2)}) copy-start(bf16[288,288]{1,0:T(8,128)(2,1)} %param.19) | copy-start | bytes 497668
  96.6 35.3 %copy-start.4 = (bf16[729,288]{0,1:T(8,128)(2,1)S(1)}, bf16[729,288]{0,1:T(8,128)(2,1)}, u32[]{:S(2)}) copy-start(bf16[729,288]{0,1:T(8,128)(2,1)} %param.14) | copy-start | bytes 1259716
  96.6 35.3 %copy-start.24 = (f32[288]{0:T(512)S(1)}, f32[288]{0:T(512)}, u32[]{:S(2)}) copy-start(f32[288]{0:T(512)} %param.20) | copy-start | bytes 3460
  96.6 285.3 %all-reduce.20.cloned.1.call-start = ((), (), s32[]{:S(2)}) async-start(), calls=%async_computation.8 | async-start | bytes 13271040 | tf_op jit(solution)/shard_map/psum | solution.py:49
  100.7 45.4 %copy-start.22 = (f32[288]{0:T(512)S(1)}, f32[288]{0:T(512)}, u32[]{:S(2)}) copy-start(f32[288]{0:T(512)} %param.21) | copy-start | bytes 3460
  100.7 45.4 %copy-start.25 = (f32[288]{0:T(512)S(1)}, f32[288]{0:T(512)}, u32[]{:S(2)}) copy-start(f32[288]{0:T(512)} %param.22) | copy-start | bytes 3460
  150.2 231.7 %copy-start.23 = (f32[1076]{0:T(1024)S(1)}, f32[1076]{0:T(1024)}, u32[]{:S(2)}) copy-start(f32[1076]{0:T(1024)} %param.24) | copy-start | bytes 12916
  150.2 275.2 %all-reduce.16.cloned.1.call-start = ((), (), s32[]{:S(2)}) async-start(), calls=%async_computation.4 | async-start | bytes 1769472 | tf_op jit(solution)/shard_map/psum | solution.py:45
  390.7 75.1 %reduce-scatter.5.cloned.1.call-start = ((), (), s32[]{:S(2)}) async-start(), calls=%async_computation.5 | async-start | bytes 1105920 | tf_op jit(solution)/shard_map/reduce_scatter | solution.py:187
  443.6 59.2 %all-gather.3.cloned.1.call-start = ((), (), s32[]{:S(2)}) async-start(), calls=%async_computation.6 | async-start | bytes 1658880 | tf_op jit(solution)/shard_map/all_gather | solution.py:205
  470.9 80.2 %all-reduce.18.cloned.1.call-start = ((), (), s32[]{:S(2)}) async-start(), calls=%async_computation.7 | async-start | bytes 3538944 | tf_op jit(solution)/shard_map/psum | solution.py:45
  474.5 28.3 %copy-start.11 = (bf16[288,864]{1,0:T(8,128)(2,1)S(1)}, bf16[288,864]{1,0:T(8,128)(2,1)}, u32[]{:S(2)}) copy-start(bf16[288,864]{1,0:T(8,128)(2,1)} %param.17) | copy-start | bytes 1492996
  476.4 29.4 %copy-start.5 = (bf16[729,288]{0,1:T(8,128)(2,1)S(1)}, bf16[729,288]{0,1:T(8,128)(2,1)}, u32[]{:S(2)}) copy-start(bf16[729,288]{0,1:T(8,128)(2,1)} %param.27) | copy-start | bytes 1259716
  505.8 3.6 copy-start.3
  505.8 4.7 copy-start.21
  505.8 4.7 copy-start.26
  505.8 155.7 %all-reduce.22.cloned.1.call-start = ((), (), s32[]{:S(2)}) async-start(), calls=%async_computation.9 | async-start | bytes 8257536 | tf_op jit(solution)/shard_map/psum | solution.py:224
  505.8 3.5 copy-start.7
  505.9 4.6 copy-start.17
  512.1 61.4 %copy-start.27 = (f32[288]{0:T(512)S(1)}, f32[288]{0:T(512)}, u32[]{:S(2)}) copy-start(f32[288]{0:T(512)} %param.26) | copy-start | bytes 3460
  (13 other events, 27.3 us)
Sparse Core Ops, SparseCore 0:
  26.1 50.9 reduce-scatter.2
  96.7 35.1 all-reduce.13
  150.4 231.4 all-reduce.19
  390.8 34.5 all-reduce.15
  443.7 22.0 reduce-scatter.4
  471.0 31.8 all-gather.2
  505.9 45.1 all-reduce.17
  554.9 106.5 all-reduce.21
where the time goes:
time: 674 us
  waiting for transfers between devices  520 us (77%)
  blocking collectives  73.1 us (11%)
  matrix products  34.8 us (5%)
  other arithmetic  21.7 us (3%)
  between operations  14.5 us (2%)
  local copies, waits for them, and re-layouts  8.61 us (1%)
    psum x1, waiting for transfers between devices, ff_total(): return lax.psum(partial_sum, 'row')  232 us
    psum x3, waiting for transfers between devices, col_total(): return lax.psum(partial_sum, 'col')  105 us
    psum x1, waiting for transfers between devices, body(): lax.psum((reduce_weight_grad, reduce_bias_grad, expand_weight_grad, expan...  84.5 us
    reduce_scatter x1, waiting for transfers between devices, body(): lax.psum_scatter(joint_part, 'row', scatter_dimension=1, tiled=True)  50.8 us
    psum x4, blocking collectives, row_totals(): return lax.psum((first, second), 'row')  49.2 us
    all_gather x1, waiting for transfers between devices, body(): joint_group = lax.all_gather(joint_grad, 'row', axis=1, tiled=True)  26.4 us
    reduce_scatter x1, waiting for transfers between devices, body(): lax.psum_scatter(contract_cols(mixed_low, merge_weight), 'row', scatter_d...  22.1 us
    all_gather x1, blocking collectives, body(): context_group = lax.all_gather(context_flat, 'row', axis=1, tiled=True)  15 us
  transfers between devices with their start and end apart: 8, of which 8 were waited for; matrix products, arithmetic and copies ran while one was open for 3% of the time, Pallas kernels for 0%

commit v1 on v0

--- a/solution.py
+++ b/solution.py
@@ -1,3 +1,4 @@
+import functools
 import jax
 import jax.numpy as jnp
 from jax import lax
@@ -10,6 +11,13 @@
 CUBIC_TERM = 0.044715
 
 
+def press_tables(buf, along_axis):
+    return lax.all_gather(buf, axis_name=along_axis).sum(axis=0)
+
+
+rails_expand = functools.partial(press_tables, along_axis="row")
+
+
 def gelu_value(preact):
     return (
         0.5
@@ -46,7 +54,7 @@
 
 
 def ff_total(partial_sum):
-    return lax.psum(partial_sum, "row")
+    return rails_expand(partial_sum)
 
 
 def norm_forward(values, norm_gain, norm_shift):

time: 674 us -> 891 us (1.32)
  waiting for transfers between devices: 520 us -> 722 us
  other arithmetic: 21.7 us -> 37.1 us
    all_gather x0 -> x2, waiting for transfers between devices: none -> 434 us  [press_tables(): return lax.all_gather(buf, axis_name=along_axis).sum(axis=0)]
    psum x1 -> x0, waiting for transfers between devices: 232 us -> none  [ff_total(): return lax.psum(partial_sum, 'row')]
    reduce_sum x0 -> x2, other arithmetic: none -> 15.6 us  [press_tables(): return lax.all_gather(buf, axis_name=along_axis).sum(axis=0)]
  transfers between devices with their start and end apart: 8 -> 9, of which waited for: 8 -> 9; matrix products, arithmetic and copies ran while one was open for 3% -> 4% of each run, Pallas kernels for 0% -> 0%
where the time goes in v1:
time: 891 us
  waiting for transfers between devices  722 us (81%)
  blocking collectives  73.3 us (8%)
  other arithmetic  37.1 us (4%)
  matrix products  34.6 us (4%)
  between operations  14.3 us (2%)
    all_gather x2, waiting for transfers between devices, press_tables(): return lax.all_gather(buf, axis_name=along_axis).sum(axis=0)  434 us
    psum x3, waiting for transfers between devices, col_total(): return lax.psum(partial_sum, 'col')  104 us
    psum x1, waiting for transfers between devices, body(): lax.psum((reduce_weight_grad, reduce_bias_grad, expand_weight_grad, expan...  84.5 us
    reduce_scatter x1, waiting for transfers between devices, body(): lax.psum_scatter(joint_part, 'row', scatter_dimension=1, tiled=True)  50.8 us
    psum x4, blocking collectives, row_totals(): return lax.psum((first, second), 'row')  49.3 us
    all_gather x1, waiting for transfers between devices, body(): joint_group = lax.all_gather(joint_grad, 'row', axis=1, tiled=True)  26.6 us
    reduce_scatter x1, waiting for transfers between devices, body(): lax.psum_scatter(contract_cols(mixed_low, merge_weight), 'row', scatter_d...  22.1 us
  transfers between devices with their start and end apart: 9, of which 9 were waited for; matrix products, arithmetic and copies ran while one was open for 4% of the time, Pallas kernels for 0%

profile of v1, /device:TPU:0, one launch (start us, length us, event | category | flops | bytes accessed | tf_op | source)
XLA Modules:
  0.0 890.5 jit_solution(6981462693697986368)
XLA Ops:
  8.5 13.7 %all-reduce.4 = (f32[729,1]{0,1:T(1,128)S(1)}, f32[729,1]{0,1:T(1,128)S(1)}) all-reduce(f32[729,1]{0,1:T(1,128)S(1)} %broadcast_in_dim.57, f32[729,1]{0,1:T(1,128)S(1)} %broadcast_in_dim.58), channel_id=1, replica_groups=mesh['dp'=2,'row'=4,'col'=4] {'row'}, use_global_device_ids=true, to_apply=%region_1.0 | all-reduce | flops 1458 | bytes 11664 | tf_op jit(solution)/shard_map/psum | solution.py:49
  22.2 3.7 fusion.43
  26.3 50.8 %reduce-scatter.3.cloned.1.call-done = f32[729,216]{0,1:T(8,128)} async-done(((f32[729,864]{0,1:T(8,128)}), f32[729,216]{0,1:T(8,128)}) %reduce-scatter.3.cloned.1.call-update) | async-done | bytes 629872 | tf_op jit(solution)/shard_map/reduce_scatter | solution.py:141
  79.5 15.0 %all-gather = bf16[729,1,288]{0,2,1:T(8,128)(2,1)S(1)} all-gather(bf16[729,1,72]{0,2,1:T(8,128)(2,1)S(1)} %bitcast.76), channel_id=2, replica_groups=mesh['dp'=2,'row'=4,'col'=4] {'row'}, dimensions={2}, use_global_device_ids=true | all-gather | bytes 524880 | tf_op jit(solution)/shard_map/all_gather | solution.py:161
  96.7 3.9 convolution_bitcast_fusion
  100.6 31.4 %all-reduce.12.cloned.1.call-done = f32[729,288]{0,1:T(8,128)} async-done(((f32[729,288]{0,1:T(8,128)}), f32[729,288]{0,1:T(8,128)}) %all-reduce.12.cloned.1.call-update) | async-done | bytes 839824 | tf_op jit(solution)/shard_map/psum | solution.py:53
  134.4 11.8 %all-reduce.3 = (f32[729,1]{0,1:T(1,128)S(1)}, f32[729,1]{0,1:T(1,128)S(1)}) all-reduce(f32[729,1]{0,1:T(1,128)S(1)} %broadcast_in_dim.60, f32[729,1]{0,1:T(1,128)S(1)} %broadcast_in_dim.61), channel_id=1, replica_groups=mesh['dp'=2,'row'=4,'col'=4] {'row'}, use_global_device_ids=true, to_apply=%region_8.9 | all-reduce | flops 1458 | bytes 11664 | tf_op jit(solution)/shard_map/psum | solution.py:49
  146.2 4.1 convolution_bitcast_fusion.1
  150.4 212.8 %all-gather.13.cloned.1.call-done = f32[4,729,1076]{1,2,0:T(8,128)} async-done(((f32[1,729,1076]{1,2,0:T(8,128)}), f32[4,729,1076]{1,2,0:T(8,128)}) %all-gather.13.cloned.1.call-update) | async-done | bytes 12550480 | tf_op jit(solution)/shard_map/all_gather | solution.py:15
  363.2 7.8 reduce_sum.191
  371.0 221.2 %all-gather.11.cloned.1.call-done = f32[4,729,1076]{1,2,0:T(8,128)} async-done(((f32[1,729,1076]{1,2,0:T(8,128)}), f32[4,729,1076]{1,2,0:T(8,128)}) %all-gather.11.cloned.1.call-update) | async-done | bytes 12550480 | tf_op jit(solution)/shard_map/all_gather | solution.py:15
  592.2 7.8 reduce_sum.190
  600.0 5.9 convert_reduce_fusion
  608.9 33.8 %all-reduce.14.cloned.1.call-done = f32[729,288]{0,1:T(8,128)} async-done(((f32[729,288]{0,1:T(8,128)}), f32[729,288]{0,1:T(8,128)}) %all-reduce.14.cloned.1.call-update) | async-done | bytes 839824 | tf_op jit(solution)/shard_map/psum | solution.py:53
  644.6 12.0 %all-reduce.2 = (f32[729,1]{0,1:T(1,128)S(1)}, f32[729,1]{0,1:T(1,128)S(1)}) all-reduce(f32[729,1]{0,1:T(1,128)S(1)} %broadcast_in_dim.63, f32[729,1]{0,1:T(1,128)S(1)} %broadcast_in_dim.62), channel_id=1, replica_groups=mesh['dp'=2,'row'=4,'col'=4] {'row'}, use_global_device_ids=true, to_apply=%region_18.19 | all-reduce | flops 1458 | bytes 11664 | tf_op jit(solution)/shard_map/psum | solution.py:49
  661.0 22.1 %reduce-scatter.5.cloned.1.call-done = f32[729,72]{0,1:T(8,128)} async-done(((f32[729,288]{0,1:T(8,128)}), f32[729,72]{0,1:T(8,128)}) %reduce-scatter.5.cloned.1.call-update) | async-done | bytes 209968 | tf_op jit(solution)/shard_map/reduce_scatter | solution.py:195
  688.2 3.4 fusion.57
  693.5 26.6 %all-gather.9.cloned.1.call-done = bf16[729,864]{0,1:T(8,128)(2,1)} async-done(((bf16[729,216]{0,1:T(8,128)(2,1)}), bf16[729,864]{0,1:T(8,128)(2,1)}) %all-gather.9.cloned.1.call-update) | async-done | bytes 1259728 | tf_op jit(solution)/shard_map/all_gather | solution.py:213
  720.1 2.9 fusion.59
  723.1 3.5 fusion.60
  729.5 38.8 %all-reduce.16.cloned.1.call-done = (f32[729,288]{0,1:T(8,128)}, f32[729,288]{0,1:T(8,128)}) async-done(((f32[729,288]{0,1:T(8,128)}, f32[729,288]{0,1:T(8,128)}), (f32[729,288]{0,1:T(8,128)}, f32[729,288]{0,1:T(8,128)})) %all-reduce.16.cloned.1.call-update) | async-done | bytes 1679632 | tf_op jit(solution)/shard_map/psum | solution.py:53
  769.9 9.0 %all-reduce.5 = (f32[288]{0:T(512)}, f32[288]{0:T(512)}, f32[1,1,144]{2,1,0:T(1,128)}, f32[288]{0:T(512)}, f32[288]{0:T(512)}, /*index=5*/f32[288]{0:T(512)}, f32[1076]{0:T(1024)}, f32[288]{0:T(512)}) all-reduce(f32[288]{0:T(512)S(1)} %get-tuple-element.64, ...), channel_id=1, replica_groups=mesh['dp'=2,'row'=4,'col'=4] {'dp'}, use_global_device_ids=true, to_apply=%region_26.27 | all-reduce | flops 2948 | bytes 23584 | tf_op jit(solution)/shard_map/psum | solution.py:232
  778.9 11.8 %all-reduce.1 = (f32[729,1]{0,1:T(1,128)S(1)}, f32[729,1]{0,1:T(1,128)S(1)}) all-reduce(f32[729,1]{0,1:T(1,128)S(1)} %broadcast_in_dim.65, f32[729,1]{0,1:T(1,128)S(1)} %broadcast_in_dim.64), channel_id=1, replica_groups=mesh['dp'=2,'row'=4,'col'=4] {'row'}, use_global_device_ids=true, to_apply=%region_24.25 | all-reduce | flops 1458 | bytes 11664 | tf_op jit(solution)/shard_map/psum | solution.py:49
  794.1 84.5 %all-reduce.18.cloned.1.call-done = (f32[288,864]{1,0:T(8,128)}, f32[288,288]{1,0:T(8,128)}, f32[288,1076]{1,0:T(8,128)}, f32[1076,288]{0,1:T(8,128)}) async-done(((f32[288,864]{1,0:T(8,128)}, f32[288,288]{1,0:T(8,128)}, f32[288,1076]{1,0:T(8,128)}, f32[1076,288]{0,1:T(8,128)}), (f32[288,864]{1,0:T(8,128)}, f32[288,288]{1,0:T(8,128)}, f32[288,1076]{1,0:T(8,128)}, ...) | async-done | bytes 3806224 | tf_op jit(solution)/shard_map/psum | solution.py:232
  (126 shorter events, 37.8 us)
Async XLA Ops:
  7.2 139.0 %copy-start = (bf16[288,1076]{1,0:T(8,128)(2,1)S(1)}, bf16[288,1076]{1,0:T(8,128)(2,1)}, u32[]{:S(2)}) copy-start(bf16[288,1076]{1,0:T(8,128)(2,1)} %param.23) | copy-start | bytes 1859332
  7.2 69.9 %reduce-scatter.3.cloned.1.call-start = ((), (), s32[]{:S(2)}) async-start(), calls=%async_computation.2 | async-start | bytes 3317760 | tf_op jit(solution)/shard_map/reduce_scatter | solution.py:141
  26.0 106.1 %all-reduce.12.cloned.1.call-start = ((), (), s32[]{:S(2)}) async-start(), calls=%async_computation.3 | async-start | bytes 1769472 | tf_op jit(solution)/shard_map/psum | solution.py:53
  78.3 16.9 %copy-start.20 = (bf16[288,288]{1,0:T(8,128)(2,1)S(1)}, bf16[288,288]{1,0:T(8,128)(2,1)}, u32[]{:S(2)}) copy-start(bf16[288,288]{1,0:T(8,128)(2,1)} %param.19) | copy-start | bytes 497668
  78.9 17.7 %copy-start.13 = (bf16[729,288]{0,1:T(8,128)(2,1)S(1)}, bf16[729,288]{0,1:T(8,128)(2,1)}, u32[]{:S(2)}) copy-start(bf16[729,288]{0,1:T(8,128)(2,1)} %param.27) | copy-start | bytes 1259716
  96.6 266.6 %all-gather.13.cloned.1.call-start = ((), (), s32[]{:S(2)}) async-start(), calls=%async_computation.8 | async-start | bytes 16588800 | tf_op jit(solution)/shard_map/all_gather | solution.py:15
  100.5 31.5 %copy-start.5 = (bf16[729,288]{0,1:T(8,128)(2,1)S(1)}, bf16[729,288]{0,1:T(8,128)(2,1)}, u32[]{:S(2)}) copy-start(bf16[729,288]{0,1:T(8,128)(2,1)} %param.14) | copy-start | bytes 1259716
  100.6 31.5 %copy-start.26 = (f32[288]{0:T(512)S(1)}, f32[288]{0:T(512)}, u32[]{:S(2)}) copy-start(f32[288]{0:T(512)} %param.20) | copy-start | bytes 3460
  100.6 45.7 %copy-start.24 = (f32[288]{0:T(512)S(1)}, f32[288]{0:T(512)}, u32[]{:S(2)}) copy-start(f32[288]{0:T(512)} %param.21) | copy-start | bytes 3460
  100.6 45.7 %copy-start.27 = (f32[288]{0:T(512)S(1)}, f32[288]{0:T(512)}, u32[]{:S(2)}) copy-start(f32[288]{0:T(512)} %param.22) | copy-start | bytes 3460
  100.6 491.7 %all-gather.11.cloned.1.call-start = ((), (), s32[]{:S(2)}) async-start(), calls=%async_computation.7 | async-start | bytes 16588800 | tf_op jit(solution)/shard_map/all_gather | solution.py:15
  150.3 492.4 %all-reduce.14.cloned.1.call-start = ((), (), s32[]{:S(2)}) async-start(), calls=%async_computation.4 | async-start | bytes 1769472 | tf_op jit(solution)/shard_map/psum | solution.py:53
  371.0 229.0 %copy-start.25 = (f32[1076]{0:T(1024)S(1)}, f32[1076]{0:T(1024)}, u32[]{:S(2)}) copy-start(f32[1076]{0:T(1024)} %param.24) | copy-start | bytes 12916
  608.8 47.8 %copy-start.14 = (bf16[729,288]{0,1:T(8,128)(2,1)S(1)}, bf16[729,288]{0,1:T(8,128)(2,1)}, u32[]{:S(2)}) copy-start(bf16[729,288]{0,1:T(8,128)(2,1)} %param.27) | copy-start | bytes 1259716
  608.9 50.8 %copy-start.21 = (bf16[288,288]{1,0:T(8,128)(2,1)S(1)}, bf16[288,288]{1,0:T(8,128)(2,1)}, u32[]{:S(2)}) copy-start(bf16[288,288]{1,0:T(8,128)(2,1)} %param.19) | copy-start | bytes 497668
  608.9 74.3 %reduce-scatter.5.cloned.1.call-start = ((), (), s32[]{:S(2)}) async-start(), calls=%async_computation.5 | async-start | bytes 1105920 | tf_op jit(solution)/shard_map/reduce_scatter | solution.py:195
  658.7 25.4 %copy-start.10 = (bf16[1,729,1,216]{1,3,2,0:T(8,128)(2,1)S(1)}, bf16[1,729,1,216]{1,3,2,0:T(8,128)(2,1)}, u32[]{:S(2)}) copy-start(bf16[1,729,1,216]{1,3,2,0:T(8,128)(2,1)} %copy-done.9) | copy-start | bytes 944788
  660.9 59.1 %all-gather.9.cloned.1.call-start = ((), (), s32[]{:S(2)}) async-start(), calls=%async_computation.6 | async-start | bytes 1658880 | tf_op jit(solution)/shard_map/all_gather | solution.py:213
  688.1 80.2 %all-reduce.16.cloned.1.call-start = ((), (), s32[]{:S(2)}) async-start(), calls=%async_computation.9 | async-start | bytes 3538944 | tf_op jit(solution)/shard_map/psum | solution.py:53
  691.6 28.5 %copy-start.11 = (bf16[288,864]{1,0:T(8,128)(2,1)S(1)}, bf16[288,864]{1,0:T(8,128)(2,1)}, u32[]{:S(2)}) copy-start(bf16[288,864]{1,0:T(8,128)(2,1)} %param.17) | copy-start | bytes 1492996
  723.0 4.8 copy-start.23
  723.0 4.7 copy-start.28
  723.0 155.7 %all-reduce.18.cloned.1.call-start = ((), (), s32[]{:S(2)}) async-start(), calls=%async_computation.10 | async-start | bytes 8257536 | tf_op jit(solution)/shard_map/psum | solution.py:232
  729.4 61.3 %copy-start.29 = (f32[288]{0:T(512)S(1)}, f32[288]{0:T(512)}, u32[]{:S(2)}) copy-start(f32[288]{0:T(512)} %param.26) | copy-start | bytes 3460
  (16 other events, 40.1 us)
Sparse Core Ops, SparseCore 0:
  26.1 50.9 reduce-scatter.2
  96.7 35.2 all-reduce.11
  133.6 229.5 all-gather.12
  364.6 227.6 all-gather.10
  609.0 33.7 all-reduce.13
  661.1 22.0 reduce-scatter.4
  688.2 31.8 all-gather.8
  723.1 45.1 all-reduce.15
  772.1 106.5 all-reduce.17
